TPU v7x, 256 devices: a whole 4x4x8 slice. The times are simulated.
256 devices in a mesh: gr: 16 (over x, y_hi, core), gc: 16 (over y_lo, z).
Axes of the slice: x: 4, y: 4 (y_hi: 2, y_lo: 2; y = y_hi * 2 + y_lo), z: 8, core: 2. Of those that a mesh axis runs over, the one named last changes fastest.
Arguments:
- border: bfloat16 [96, 768, 2048], P('gc', None, 'gr'), may hold values from -1 to 1
- row_scale: float32 [96, 768], P('gc'), may hold values from 0.1 to 10
- block_pick: int32 [96, 16], replicated, may hold values from 0 to 3
- given_diag: float32 [8192], replicated, may hold values from 0.5 to 4
Outputs:
- factored: float32 [8192, 8192], P('gr', 'gc')
All inputs are finite; a program needn't handle non-finite values.
Results may differ from a plain program's by a relative error of at most 0.00097.
Values may be sent and summed in bfloat16 or wider, within the bound.
No kernel may reach another device: no remote copies, remote signals or barrier semaphores. Data moves between devices by JAX's collectives and lax.ppermute only.
A program may use at most 128 MiB of HBM per device.

v0:
```python
import jax
import jax.numpy as jnp
from jax import lax
from jax.sharding import PartitionSpec as P

N = 8192
BLK = 128
NWIN = 16
PW = 256
PANELS = 2


def broadcast(x, axis, root):
    mine = lax.axis_index(axis) == root
    return lax.psum(jnp.where(mine, x, jnp.zeros_like(x)), axis)


def place_tiles(row_pick, col_pick, gram_tiles, span_count):
    positions = jnp.arange(span_count, dtype=jnp.int32)
    rows_hot = (row_pick[:, :, None] == positions[None, None, :]).astype(jnp.float32)
    cols_hot = (col_pick[:, :, None] == positions[None, None, :]).astype(jnp.float32)
    pair_hot = jnp.einsum("sam,sbn->sambn", rows_hot, cols_hot)
    return jnp.einsum("sambn,saxby->amxbny", pair_hot, gram_tiles, precision=lax.Precision.HIGHEST)


def body(border, row_scale, block_pick, given_diag):
    grid_rows = lax.axis_size("gr")
    grid_cols = lax.axis_size("gc")
    row_index = lax.axis_index("gr")
    col_index = lax.axis_index("gc")
    scen_here = border.shape[0]
    row_windows = NWIN // grid_rows
    col_windows = NWIN // grid_cols
    span_count = N // (BLK * NWIN)
    local_rows = N // grid_rows
    local_cols = N // grid_cols
    scaled = (jnp.sqrt(row_scale)[:, :, None] * border).astype(jnp.bfloat16)
    gram_rows = jnp.einsum(
        "srx,sry->sxy",
        scaled,
        lax.all_gather(scaled, "gr", axis=2, tiled=True),
        preferred_element_type=jnp.float32,
    )
    gram_tiles = gram_rows.reshape(scen_here, row_windows, BLK, NWIN, BLK)
    received = lax.all_to_all(gram_tiles, "gc", split_axis=3, concat_axis=0, tiled=True)
    row_pick = lax.dynamic_slice_in_dim(block_pick, row_index * row_windows, row_windows, 1)
    col_pick = lax.dynamic_slice_in_dim(block_pick, col_index * col_windows, col_windows, 1)
    placed = place_tiles(row_pick, col_pick, received, span_count)
    assembled = placed.reshape(local_rows, local_cols)
    row_global = row_index * local_rows + jnp.arange(local_rows, dtype=jnp.int32)
    col_global = col_index * local_cols + jnp.arange(local_cols, dtype=jnp.int32)
    diag_here = lax.dynamic_slice_in_dim(given_diag, row_index * local_rows, local_rows, 0)
    factored = assembled + jnp.where(
        row_global[:, None] == col_global[None, :], diag_here[:, None], 0.0
    )
    row_ratio = grid_rows // grid_cols
    for panel_index in range(PANELS):
        first_col = panel_index * PW
        past_col = first_col + PW
        corner = broadcast(factored[first_col:past_col, first_col:past_col], "gr", 0)
        chol_block = jnp.linalg.cholesky(corner)
        solved = jax.scipy.linalg.solve_triangular(
            chol_block, factored[:, first_col:past_col].T, lower=True
        ).T
        padded = jnp.zeros((local_rows, PW), jnp.float32).at[first_col:past_col].set(chol_block)
        row_inside = (row_global >= first_col) & (row_global < past_col)
        solved = jnp.where(
            (row_global >= past_col)[:, None], solved, jnp.where(row_inside[:, None], padded, 0.0)
        )
        panel_rows = broadcast(solved, "gc", 0)
        col_inside = (col_global >= first_col) & (col_global < past_col)
        pieces = broadcast(panel_rows, "gr", col_index * row_ratio + 0)
        product = jnp.dot(
            panel_rows,
            pieces.T,
            precision=lax.Precision.HIGHEST,
            preferred_element_type=jnp.float32,
        )
        trailing = (row_global >= past_col)[:, None] & (col_global >= past_col)[None, :]
        placed_cols = (
            jnp.zeros((local_rows, local_cols), jnp.float32)
            .at[:, first_col:past_col]
            .set(panel_rows)
        )
        factored = jnp.where(trailing, factored - product, factored)
        factored = jnp.where(col_inside[None, :], placed_cols, factored)
        factored = jnp.where(row_inside[:, None] & (col_global >= past_col)[None, :], 0.0, factored)
    return factored


def solution(mesh):
    in_specs = (P("gc", None, "gr"), P("gc", None), P(), P())
    out_specs = P("gr", "gc")
    return jax.shard_map(body, mesh=mesh, in_specs=in_specs, out_specs=out_specs, check_vma=False)
```

profile of v0, /device:TPU:1, one launch (start us, length us, event | category | flops | bytes accessed | tf_op | source)
XLA Modules:
  0.0 1326.2 jit_solution(5797193775737873356)
XLA Ops:
  6.5 0.7 sqrt.3
  7.3 2.7 multiply_convert_fusion
  10.0 142.5 %all-gather.2.cloned.1.call-done = bf16[6,768,2048]{2,1,0:T(8,128)(2,1)} async-done(((bf16[6,768,128]{2,1,0:T(8,128)(2,1)}), bf16[6,768,2048]{2,1,0:T(8,128)(2,1)}) %all-gather.2.cloned.1.call-update) | async-done | bytes 18874384 | tf_op jit(solution)/shard_map/all_gather | solution.py:41
  152.5 8.3 fusion.63
  160.8 1.5 copy.63
  162.2 4.6 copy.39
  166.8 6.9 all-to-all-start
  173.8 0.8 dynamic_slice.11
  174.6 0.8 fusion.59
  175.4 138.1 %all-to-all-done = f32[6,1,128,16,128]{4,2,0,1,3:T(8,128)} async-done(((f32[6,1,128,16,128]{4,2,0,1,3:T(8,128)}), f32[6,1,128,16,128]{4,2,0,1,3:T(8,128)}, u32[]{:S(2)}, u32[]{:S(2)}) %all-to-all-start) | async-done | bytes 6291488 | tf_op jit(solution)/shard_map/all_to_all | solution.py:45
  313.5 9.6 fusion.2
  323.8 0.7 slice_select_fusion.1
  324.8 145.2 %all-reduce.12.cloned.1.call-done = f32[256,256]{0,1:T(8,128)} async-done(((f32[256,256]{0,1:T(8,128)}), f32[256,256]{0,1:T(8,128)}) %all-reduce.12.cloned.1.call-update) | async-done | bytes 262160 | tf_op jit(solution)/shard_map/psum | solution.py:15
  470.1 1.1 copy.42
  471.1 1.0 fusion.18
  472.1 11.7 cholesky.130
  484.0 9.8 custom-call.13
  494.4 11.7 cholesky.147
  506.2 0.6 compare_reduce_fusion.3
  506.9 0.7 compare_reduce_fusion.2
  509.1 4.6 while.8
  510.0 1.4 dynamic-slice.50
  512.1 1.4 dynamic-slice.50
  513.7 19.7 %custom-call.14 = f32[2,128,128]{1,2,0:T(8,128)S(1)} custom-call(f32[2,128,128]{2,1,0:T(8,128)S(1)} %get-tuple-element.69), custom_call_target="InvertDiagBlocksLowerTriangular" | custom-call | tf_op jit(solution)/shard_map/jit(_solve_triangular)/triangular_solve | solution.py:62
  534.7 0.9 fusion.10
  535.6 0.7 compare_reduce_fusion.4
  536.3 126.2 %all-reduce.14.cloned.1.call-done = f32[512,256]{0,1:T(8,128)} async-done(((f32[512,256]{0,1:T(8,128)}), f32[512,256]{0,1:T(8,128)}) %all-reduce.14.cloned.1.call-update) | async-done | bytes 524304 | tf_op jit(solution)/shard_map/psum | solution.py:15
  662.5 2.7 broadcast_select_fusion.2
  665.2 153.1 %all-reduce.16.cloned.1.call-done = f32[512,256]{0,1:T(8,128)} async-done(((f32[512,256]{0,1:T(8,128)}), f32[512,256]{0,1:T(8,128)}) %all-reduce.16.cloned.1.call-update) | async-done | bytes 524304 | tf_op jit(solution)/shard_map/psum | solution.py:15
  818.3 2.5 fusion.8
  820.8 0.7 slice_select_fusion
  821.7 145.3 %all-reduce.18.cloned.1.call-done = f32[256,256]{0,1:T(8,128)} async-done(((f32[256,256]{0,1:T(8,128)}), f32[256,256]{0,1:T(8,128)}) %all-reduce.18.cloned.1.call-update) | async-done | bytes 262160 | tf_op jit(solution)/shard_map/psum | solution.py:15
  966.9 1.1 copy.48
  968.0 1.0 fusion.17
  969.0 11.7 cholesky.164
  980.9 9.8 custom-call.15
  991.3 11.7 cholesky.181
  1003.8 0.7 compare_reduce_fusion
  1005.9 4.6 while.9
  1006.8 1.4 dynamic-slice.52
  1009.0 1.4 dynamic-slice.52
  1010.5 19.7 %custom-call.16 = f32[2,128,128]{1,2,0:T(8,128)S(1)} custom-call(f32[2,128,128]{2,1,0:T(8,128)S(1)} %get-tuple-element.70), custom_call_target="InvertDiagBlocksLowerTriangular" | custom-call | tf_op jit(solution)/shard_map/jit(_solve_triangular)/triangular_solve | solution.py:62
  1031.5 0.9 fusion.12
  1032.5 126.9 %all-reduce.20.cloned.1.call-done = f32[512,256]{0,1:T(8,128)} async-done(((f32[512,256]{0,1:T(8,128)}), f32[512,256]{0,1:T(8,128)}) %all-reduce.20.cloned.1.call-update) | async-done | bytes 524304 | tf_op jit(solution)/shard_map/psum | solution.py:15
  1159.3 0.8 broadcast_select_fusion
  1160.2 154.7 %all-reduce.22.cloned.1.call-done = f32[512,256]{0,1:T(8,128)} async-done(((f32[512,256]{0,1:T(8,128)}), f32[512,256]{0,1:T(8,128)}) %all-reduce.22.cloned.1.call-update) | async-done | bytes 524304 | tf_op jit(solution)/shard_map/psum | solution.py:15
  1315.0 2.7 fusion.6
  1317.6 1.3 copy.54
  (79 shorter events, 9.3 us)
Async XLA Ops:
  6.5 146.0 %all-gather.2.cloned.1.call-start = ((), (), s32[]{:S(2)}) async-start(), calls=%async_computation.1 | async-start | bytes 20054016 | tf_op jit(solution)/shard_map/all_gather | solution.py:41
  166.8 146.7 %all-to-all-start = ((f32[6,1,128,16,128]{4,2,0,1,3:T(8,128)}), f32[6,1,128,16,128]{4,2,0,1,3:T(8,128)}, u32[]{:S(2)}, u32[]{:S(2)}) async-start(f32[6,1,128,16,128]{4,2,0,1,3:T(8,128)} %copy.39), calls=%async_computation | async-start | bytes 12582912 | tf_op jit(solution)/shard_map/all_to_all | solution.py:45
  173.7 296.3 %all-reduce.12.cloned.1.call-start = ((), (), s32[]{:S(2)}) async-start(), calls=%async_computation.2 | async-start | bytes 524288 | tf_op jit(solution)/shard_map/psum | solution.py:15
  324.6 337.9 %all-reduce.14.cloned.1.call-start = ((), (), s32[]{:S(2)}) async-start(), calls=%async_computation.3 | async-start | bytes 1048576 | tf_op jit(solution)/shard_map/psum | solution.py:15
  535.5 282.8 %all-reduce.16.cloned.1.call-start = ((), (), s32[]{:S(2)}) async-start(), calls=%async_computation.4 | async-start | bytes 1048576 | tf_op jit(solution)/shard_map/psum | solution.py:15
  665.2 301.8 %all-reduce.18.cloned.1.call-start = ((), (), s32[]{:S(2)}) async-start(), calls=%async_computation.5 | async-start | bytes 524288 | tf_op jit(solution)/shard_map/psum | solution.py:15
  821.6 337.8 %all-reduce.20.cloned.1.call-start = ((), (), s32[]{:S(2)}) async-start(), calls=%async_computation.6 | async-start | bytes 1048576 | tf_op jit(solution)/shard_map/psum | solution.py:15
  1032.4 282.6 %all-reduce.22.cloned.1.call-start = ((), (), s32[]{:S(2)}) async-start(), calls=%async_computation.7 | async-start | bytes 1048576 | tf_op jit(solution)/shard_map/psum | solution.py:15
Sparse Core Ops, SparseCore 0:
  10.1 142.3 all-gather.1
  324.7 145.3 all-reduce.11
  535.7 126.7 all-reduce.13
  665.3 152.9 all-reduce.15
  821.7 145.2 all-reduce.17
  1032.5 126.7 all-reduce.19
  1162.0 152.9 all-reduce.21
where the time goes:
time: 1330 us
  waiting for transfers between devices  1130 us (85%)
  other arithmetic  121 us (9%)
  matrix products  26.5 us (2%)
  local copies, waits for them, and re-layouts  21.6 us (2%)
  between operations  17 us (1%)
    psum x6, waiting for transfers between devices, broadcast(): return lax.psum(jnp.where(mine, x, jnp.zeros_like(x)), axis)  851 us
    all_gather x1, waiting for transfers between devices, body(): lax.all_gather(scaled, 'gr', axis=2, tiled=True)  143 us
    all_to_all x1, waiting for transfers between devices, body(): lax.all_to_all(gram_tiles, 'gc', split_axis=3, concat_axis=0, tiled=True)  138 us
    another operation x14, other arithmetic, body(): chol_block = jnp.linalg.cholesky(corner)  69.3 us
    another operation x3, other arithmetic, body(): jax.scipy.linalg.solve_triangular(chol_block, factored[:, first_col:past_...  39.4 us
  transfers between devices with their start and end apart: 8, of which 8 were waited for; matrix products, arithmetic and copies ran while one was open for 0% of the time, Pallas kernels for 0%

commit v1 on v0

--- a/solution.py
+++ b/solution.py
@@ -12,7 +12,7 @@
 
 def broadcast(x, axis, root):
     mine = lax.axis_index(axis) == root
-    return lax.psum(jnp.where(mine, x, jnp.zeros_like(x)), axis)
+    return jnp.sum(lax.all_gather(jnp.where(mine, x, jnp.zeros_like(x)), axis), axis=0)
 
 
 def place_tiles(row_pick, col_pick, gram_tiles, span_count):

time: 1330 us -> 969 us (0.73)
  waiting for transfers between devices: 1130 us -> 753 us
  other arithmetic: 121 us -> 139 us
    psum x6 -> x0, waiting for transfers between devices: 851 us -> none  [broadcast(): return lax.psum(jnp.where(mine, x, jnp.zeros_like(x)), axis)]
    all_gather x0 -> x6, waiting for transfers between devices: none -> 472 us  [broadcast(): lax.all_gather(jnp.where(mine, x, jnp.zeros_like(x)), axis)]
    reduce_sum x0 -> x6, other arithmetic: none -> 20.9 us  [broadcast(): jnp.sum(lax.all_gather(jnp.where(mine, x, jnp.zeros_like(x)), axis), axis=0)]
where the time goes in v1:
time: 969 us; the launch traced here: 961 us
  waiting for transfers between devices  753 us (78%)
  other arithmetic  139 us (14%)
  matrix products  26.2 us (3%)
  local copies, waits for them, and re-layouts  17.3 us (2%)
  between operations  17.1 us (2%)
    all_gather x6, waiting for transfers between devices, broadcast(): lax.all_gather(jnp.where(mine, x, jnp.zeros_like(x)), axis)  472 us
    all_gather x1, waiting for transfers between devices, body(): lax.all_gather(scaled, 'gr', axis=2, tiled=True)  143 us
    all_to_all x1, waiting for transfers between devices, body(): lax.all_to_all(gram_tiles, 'gc', split_axis=3, concat_axis=0, tiled=True)  138 us
    another operation x14, other arithmetic, body(): chol_block = jnp.linalg.cholesky(corner)  69.3 us
    another operation x3, other arithmetic, body(): jax.scipy.linalg.solve_triangular(chol_block, factored[:, first_col:past_...  39.4 us
    reduce_sum x6, other arithmetic, broadcast(): jnp.sum(lax.all_gather(jnp.where(mine, x, jnp.zeros_like(x)), axis), axis=0)  20.9 us
  transfers between devices with their start and end apart: 8, of which 8 were waited for; matrix products, arithmetic and copies ran while one was open for 0% of the time, Pallas kernels for 0%

profile of v1, /device:TPU:1, one launch (start us, length us, event | category | flops | bytes accessed | tf_op | source)
XLA Modules:
  0.0 961.2 jit_solution(10918788772692299019)
XLA Ops:
  6.5 0.7 sqrt.3
  7.3 2.7 multiply_convert_fusion
  10.0 142.5 %all-gather.14.cloned.1.call-done = bf16[6,768,2048]{2,1,0:T(8,128)(2,1)} async-done(((bf16[6,768,128]{2,1,0:T(8,128)(2,1)}), bf16[6,768,2048]{2,1,0:T(8,128)(2,1)}) %all-gather.14.cloned.1.call-update) | async-done | bytes 18874384 | tf_op jit(solution)/shard_map/all_gather | solution.py:41
  152.5 8.3 fusion.63
  160.8 1.5 copy.44
  162.2 4.6 copy.25
  166.8 6.9 all-to-all-start
  173.8 0.8 dynamic_slice.11
  174.6 0.8 fusion.59
  175.3 138.1 %all-to-all-done = f32[6,1,128,16,128]{4,2,0,1,3:T(8,128)} async-done(((f32[6,1,128,16,128]{4,2,0,1,3:T(8,128)}), f32[6,1,128,16,128]{4,2,0,1,3:T(8,128)}, u32[]{:S(2)}, u32[]{:S(2)}) %all-to-all-start) | async-done | bytes 6291488 | tf_op jit(solution)/shard_map/all_to_all | solution.py:45
  313.5 9.6 %fusion.2 = f32[1,4,128,1,4,128]{5,4,1,2,3,0:T(4,128)S(1)} fusion(f32[96,128,128,1]{2,1,0,3:T(8,128)} %bitcast.3, f32[96,4]{0,1:T(4,128)S(1)} %get-tuple-element.114, f32[96,4]{0,1:T(4,128)S(1)} %get-tuple-element.113), kind=kOutput, calls=%fused_computation.9 | convolution fusion | flops 301991424 | bytes 7343104 | tf_op jit(solution)/shard_map/sambn,saxby->amxbny/dot_general | solution.py:23
  323.5 0.7 slice_select_fusion.1
  324.6 63.0 %all-gather.16.cloned.1.call-done = f32[4096,256]{1,0:T(8,128)} async-done(((f32[256,256]{1,0:T(8,128)}), f32[4096,256]{1,0:T(8,128)}) %all-gather.16.cloned.1.call-update) | async-done | bytes 4194320 | tf_op jit(solution)/shard_map/all_gather | solution.py:15
  387.6 2.5 reduce_sum.54
  390.3 11.7 %cholesky.130 = f32[128,128]{1,0:T(8,128)S(1)} custom-call(f32[128,128]{1,0:T(8,128)S(1)} %cholesky.194), custom_call_target="Cholesky" | custom-call | tf_op jit(solution)/shard_map/jit(cholesky)/cholesky | solution.py:61
  402.1 9.8 %custom-call.13 = f32[1,128,128]{1,2,0:T(8,128)S(1)} custom-call(f32[1,128,128]{2,1,0:T(8,128)S(1)} %get-tuple-element.106), custom_call_target="InvertDiagBlocksLowerTriangular" | custom-call | tf_op jit(solution)/shard_map/jit(cholesky)/cholesky | solution.py:61
  412.4 11.7 %cholesky.147 = f32[128,128]{1,0:T(8,128)S(1)} custom-call(f32[128,128]{1,0:T(8,128)S(1)} %convolution_subtract_fusion.3), custom_call_target="Cholesky" | custom-call | tf_op jit(solution)/shard_map/jit(cholesky)/cholesky | solution.py:61
  424.8 0.7 compare_reduce_fusion.2
  427.0 4.3 while.8
  427.8 1.4 bitcast_dynamic-update-slice_fusion.4
  429.9 1.4 bitcast_dynamic-update-slice_fusion.4
  431.3 19.7 %custom-call.14 = f32[2,128,128]{1,2,0:T(8,128)S(1)} custom-call(f32[2,128,128]{2,1,0:T(8,128)S(1)} %get-tuple-element.69), custom_call_target="InvertDiagBlocksLowerTriangular" | custom-call | tf_op jit(solution)/shard_map/jit(_solve_triangular)/triangular_solve | solution.py:62
  452.5 0.9 fusion.10
  453.6 0.7 compare_reduce_fusion.4
  454.2 98.6 %all-gather.18.cloned.1.call-done = f32[8192,256]{1,0:T(8,128)} async-done(((f32[512,256]{1,0:T(8,128)}), f32[8192,256]{1,0:T(8,128)}) %all-gather.18.cloned.1.call-update) | async-done | bytes 8388624 | tf_op jit(solution)/shard_map/all_gather | solution.py:15
  552.9 4.0 reduce_sum.55
  556.8 1.7 broadcast_select_fusion.2
  558.7 76.2 %all-gather.20.cloned.1.call-done = f32[8192,256]{1,0:T(8,128)} async-done(((f32[512,256]{1,0:T(8,128)}), f32[8192,256]{1,0:T(8,128)}) %all-gather.20.cloned.1.call-update) | async-done | bytes 8388624 | tf_op jit(solution)/shard_map/all_gather | solution.py:15
  634.9 4.0 reduce_sum.56
  638.8 2.3 fusion.8
  641.2 0.7 slice_select_fusion
  642.3 58.9 %all-gather.22.cloned.1.call-done = f32[4096,256]{1,0:T(8,128)} async-done(((f32[256,256]{1,0:T(8,128)}), f32[4096,256]{1,0:T(8,128)}) %all-gather.22.cloned.1.call-update) | async-done | bytes 4194320 | tf_op jit(solution)/shard_map/all_gather | solution.py:15
  701.2 2.5 reduce_sum.57
  703.9 11.7 %cholesky.164 = f32[128,128]{1,0:T(8,128)S(1)} custom-call(f32[128,128]{1,0:T(8,128)S(1)} %cholesky.197), custom_call_target="Cholesky" | custom-call | tf_op jit(solution)/shard_map/jit(cholesky)/cholesky | solution.py:61
  715.7 9.8 %custom-call.15 = f32[1,128,128]{1,2,0:T(8,128)S(1)} custom-call(f32[1,128,128]{2,1,0:T(8,128)S(1)} %get-tuple-element.102), custom_call_target="InvertDiagBlocksLowerTriangular" | custom-call | tf_op jit(solution)/shard_map/jit(cholesky)/cholesky | solution.py:61
  726.0 11.7 %cholesky.181 = f32[128,128]{1,0:T(8,128)S(1)} custom-call(f32[128,128]{1,0:T(8,128)S(1)} %convolution_subtract_fusion.2), custom_call_target="Cholesky" | custom-call | tf_op jit(solution)/shard_map/jit(cholesky)/cholesky | solution.py:61
  738.4 0.7 compare_reduce_fusion
  740.5 4.4 while.9
  741.5 1.4 bitcast_dynamic-update-slice_fusion.5
  743.5 1.4 bitcast_dynamic-update-slice_fusion.5
  744.9 19.7 %custom-call.16 = f32[2,128,128]{1,2,0:T(8,128)S(1)} custom-call(f32[2,128,128]{2,1,0:T(8,128)S(1)} %get-tuple-element.70), custom_call_target="InvertDiagBlocksLowerTriangular" | custom-call | tf_op jit(solution)/shard_map/jit(_solve_triangular)/triangular_solve | solution.py:62
  766.2 0.9 fusion.12
  767.2 99.3 %all-gather.24.cloned.1.call-done = f32[8192,256]{1,0:T(8,128)} async-done(((f32[512,256]{1,0:T(8,128)}), f32[8192,256]{1,0:T(8,128)}) %all-gather.24.cloned.1.call-update) | async-done | bytes 8388624 | tf_op jit(solution)/shard_map/all_gather | solution.py:15
  866.5 4.0 reduce_sum.58
  870.5 0.8 broadcast_select_fusion
  871.3 76.2 %all-gather.26.cloned.1.call-done = f32[8192,256]{1,0:T(8,128)} async-done(((f32[512,256]{1,0:T(8,128)}), f32[8192,256]{1,0:T(8,128)}) %all-gather.26.cloned.1.call-update) | async-done | bytes 8388624 | tf_op jit(solution)/shard_map/all_gather | solution.py:15
  947.6 4.0 reduce_sum.59
  951.6 2.3 fusion.6
  (68 shorter events, 9.8 us)
Async XLA Ops:
  6.5 146.0 %all-gather.14.cloned.1.call-start = ((), (), s32[]{:S(2)}) async-start(), calls=%async_computation.1 | async-start | bytes 20054016 | tf_op jit(solution)/shard_map/all_gather | solution.py:41
  166.8 146.7 %all-to-all-start = ((f32[6,1,128,16,128]{4,2,0,1,3:T(8,128)}), f32[6,1,128,16,128]{4,2,0,1,3:T(8,128)}, u32[]{:S(2)}, u32[]{:S(2)}) async-start(f32[6,1,128,16,128]{4,2,0,1,3:T(8,128)} %copy.25), calls=%async_computation | async-start | bytes 12582912 | tf_op jit(solution)/shard_map/all_to_all | solution.py:45
  173.7 213.9 %all-gather.16.cloned.1.call-start = ((), (), s32[]{:S(2)}) async-start(), calls=%async_computation.2 | async-start | bytes 4456448 | tf_op jit(solution)/shard_map/all_gather | solution.py:15
  324.3 228.6 %all-gather.18.cloned.1.call-start = ((), (), s32[]{:S(2)}) async-start(), calls=%async_computation.3 | async-start | bytes 8912896 | tf_op jit(solution)/shard_map/all_gather | solution.py:15
  453.5 181.4 %all-gather.20.cloned.1.call-start = ((), (), s32[]{:S(2)}) async-start(), calls=%async_computation.4 | async-start | bytes 8912896 | tf_op jit(solution)/shard_map/all_gather | solution.py:15
  558.6 142.6 %all-gather.22.cloned.1.call-start = ((), (), s32[]{:S(2)}) async-start(), calls=%async_computation.5 | async-start | bytes 4456448 | tf_op jit(solution)/shard_map/all_gather | solution.py:15
  641.9 224.5 %all-gather.24.cloned.1.call-start = ((), (), s32[]{:S(2)}) async-start(), calls=%async_computation.6 | async-start | bytes 8912896 | tf_op jit(solution)/shard_map/all_gather | solution.py:15
  767.1 180.4 %all-gather.26.cloned.1.call-start = ((), (), s32[]{:S(2)}) async-start(), calls=%async_computation.7 | async-start | bytes 8912896 | tf_op jit(solution)/shard_map/all_gather | solution.py:15
Sparse Core Ops, SparseCore 0:
  10.1 142.3 all-gather.13
  324.4 63.1 all-gather.15
  453.6 99.1 all-gather.17
  558.7 76.1 all-gather.19
  642.1 59.1 all-gather.21
  767.2 99.1 all-gather.23
  871.4 76.1 all-gather.25
